TPU v7x, 32 devices: a whole 2x2x4 slice. The times are simulated.
32 devices in a mesh: grp: 2 (over core), aux: 8 (over z, x), tr: 2 (over y).
Axes of the slice: x: 2, y: 2, z: 4, core: 2. Of those that a mesh axis runs over, the one named last changes fastest.
Arguments:
- trial_vectors: float32 [64, 8, 512], P('aux', None, 'tr'), may hold values from -6 to 6
- energy_val: float32 [64], P('aux'), may hold values from -1 to -0.2
- energy_cond: float32 [512], P('tr'), may hold values from 0.2 to 2
- coef_occ: bfloat16 [512, 64, 64], P('aux'), may hold values from -0.75 to 0.75
- coef_virt: bfloat16 [512, 512, 512], P('aux', 'tr'), may hold values from -0.01171875 to 0.01171875
- pair_coef: bfloat16 [64, 512, 512], P('aux', 'tr'), may hold values from -0.03125 to 0.03125
- live_aux: int32 [8], P('aux'), may hold values from 16 to 64, as said below
Outputs:
- applied: float32 [64, 8, 512], P('aux', None, 'tr')
- intersection: float32 [8, 8], replicated
Inputs may be any that keep to these rules, and one draw needn't show every extreme that they name: `live_aux`: equals 64 on at least one shard.
All inputs are finite; a program needn't handle non-finite values.
Results may differ from a plain program's by a relative error of at most 0.0048.
Values may be sent and summed in bfloat16 or wider, within the bound.
A program may use at most 64 MiB of HBM per device.

v0:
```python
import math
import jax
import jax.numpy as jnp
from jax import lax
from jax.sharding import PartitionSpec as P

V = 64
C = 512


def apply_hamiltonian(vectors, energy_gap, coef_occ, coef_virt, pair_coef, live_aux):
    rounded = vectors.astype(jnp.bfloat16)
    gathered = lax.all_gather(rounded, "aux", axis=0, tiled=True)
    group_index = lax.axis_index("grp")
    slots = coef_occ.shape[0]
    live_count = live_aux[0]
    zero_slot = jnp.zeros((), jnp.int32)
    range_high = jnp.where(group_index == 0, live_count, zero_slot)
    block_size = math.gcd(slots, 8)
    first_block = zero_slot // block_size
    last_block = (range_high + block_size - 1) // block_size
    full_vectors = gathered.shape[1]
    full_cond = coef_virt.shape[2]

    def one_block(block_index, running):
        slot_start = block_index * block_size
        piece_occ = lax.dynamic_slice_in_dim(coef_occ, slot_start, block_size, 0)
        piece_virt = lax.dynamic_slice_in_dim(coef_virt, slot_start, block_size, 0)
        slot_ids = slot_start + lax.iota(jnp.int32, block_size)
        keep_mask = ((slot_ids >= zero_slot) & (slot_ids < range_high)).astype(jnp.float32)
        blended = jnp.einsum(
            "puv,vkc->pukc", piece_occ, gathered, preferred_element_type=jnp.float32
        )
        blended = (blended * keep_mask[:, None, None, None]).astype(jnp.bfloat16)
        return running + jnp.einsum(
            "pukc,pcd->ukd", blended, piece_virt, preferred_element_type=jnp.float32
        )

    zero_term = jnp.zeros((gathered.shape[0], full_vectors, full_cond), jnp.float32)
    direct_term = lax.fori_loop(first_block, last_block, one_block, zero_term)
    direct_term = lax.psum_scatter(direct_term, "tr", scatter_dimension=2, tiled=True)
    direct_term = lax.psum_scatter(direct_term, "aux", scatter_dimension=0, tiled=True)
    is_exchange = group_index == 1
    projection = lax.cond(
        is_exchange,
        lambda: jnp.einsum("vcp,vkc->kp", pair_coef, rounded, preferred_element_type=jnp.float32),
        lambda: jnp.zeros((vectors.shape[1], pair_coef.shape[2]), jnp.float32),
    )
    projection = lax.psum(projection, ("aux", "tr"))
    projection_b = projection.astype(jnp.bfloat16)
    exchange_term = lax.cond(
        is_exchange,
        lambda: jnp.einsum(
            "vcp,kp->vkc", pair_coef, projection_b, preferred_element_type=jnp.float32
        ),
        lambda: jnp.zeros(vectors.shape, jnp.float32),
    )
    combined = lax.psum(direct_term + exchange_term, "grp")
    return energy_gap[:, None, :] * vectors + combined


def body(trial_vectors, energy_val, energy_cond, coef_occ, coef_virt, pair_coef, live_aux):
    energy_gap = energy_cond[None, :] - energy_val[:, None]
    applied_first = apply_hamiltonian(
        trial_vectors, energy_gap, coef_occ, coef_virt, pair_coef, live_aux
    )
    partial_intersection = jnp.einsum(
        "vkc,vjc->kj", trial_vectors, applied_first, precision=lax.Precision.HIGHEST
    )
    intersection = lax.psum(partial_intersection, ("aux", "tr")) / (V * C)
    residual = applied_first - jnp.einsum(
        "vkc,kj->vjc", trial_vectors, intersection, precision=lax.Precision.HIGHEST
    )
    correction = residual / energy_gap[:, None, :]
    applied = apply_hamiltonian(correction, energy_gap, coef_occ, coef_virt, pair_coef, live_aux)
    return (applied, intersection)


def solution(mesh):
    in_specs = (
        P("aux", None, "tr"),
        P("aux"),
        P("tr"),
        P("aux", None, None),
        P("aux", "tr", None),
        P("aux", "tr", None),
        P("aux"),
    )
    out_specs = (P("aux", None, "tr"), P())
    return jax.shard_map(body, mesh=mesh, in_specs=in_specs, out_specs=out_specs, check_vma=False)
```

profile of v0, /device:TPU:0, one launch (start us, length us, event | category | flops | bytes accessed | tf_op | source)
XLA Modules:
  0.0 438.0 jit_solution(5328799634057705139)
XLA Ops:
  8.7 32.5 %all_gather.6 = bf16[64,8,256]{2,1,0:T(8,128)(2,1)S(1)} all-gather(bf16[8,8,256]{2,1,0:T(8,128)(2,1)S(1)} %convert_element_type.40), channel_id=1, replica_groups=mesh['grp'=2,'aux'=8,'tr'=2] {'aux'}, dimensions={0}, use_global_device_ids=true | all-gather | bytes 294912 | tf_op jit(solution)/shard_map/all_gather | solution.py:13
  41.4 46.7 %while.20 = (s32[]{:T(128)}, f32[64,8,512]{2,1,0:T(8,128)S(1)}, s32[]{:T(128)}, bf16[64,64,64]{2,1,0:T(8,128)(2,1)}, bf16[64,8,256]{2,1,0:T(8,128)(2,1)S(1)}, /*...) while((s32[]{:T(128)}, f32[64,8,512]{2,1,0:T(8,128)S(1)}, ...), condition=%wide.region_1.2_spmd, body=%wide.region_0.1_spmd.sunk | while | flops 1210318848 | bytes 12976363 | solution.py:40
  43.2 4.2 fusion.78
  49.0 4.2 fusion.78
  54.8 4.2 fusion.78
  60.7 4.2 fusion.78
  66.5 4.2 fusion.78
  72.3 4.2 fusion.78
  78.1 4.2 fusion.78
  83.9 4.2 fusion.78
  89.2 18.8 %reduce-scatter.5.cloned.1.call-done = f32[64,8,256]{2,1,0:T(8,128)} async-done(((f32[64,8,512]{2,1,0:T(8,128)}), f32[64,8,256]{2,1,0:T(8,128)}) %reduce-scatter.5.cloned.1.call-update) | async-done | bytes 524304 | tf_op jit(solution)/shard_map/reduce_scatter | solution.py:41
  108.1 75.8 %psum.35 = bf16[8,512]{1,0:T(8,128)(2,1)S(1)} all-reduce(f32[8,512]{1,0:T(8,128)S(1)} %get-tuple-element.306), channel_id=1, replica_groups=mesh['grp'=2,'aux'=8,'tr'=2] {'aux','tr'}, use_global_device_ids=true, to_apply=%region_6.7 | all-reduce | flops 4096 | bytes 24576 | tf_op jit(solution)/shard_map/psum | solution.py:49
  185.6 13.6 %all-reduce.3.cloned.1.call-done = f32[8,8,256]{2,1,0:T(8,128)} async-done(((f32[8,8,256]{2,1,0:T(8,128)}), f32[8,8,256]{2,1,0:T(8,128)}) %all-reduce.3.cloned.1.call-update) | async-done | bytes 65552 | tf_op jit(solution)/shard_map/psum | solution.py:58
  200.3 42.1 %psum.37 = f32[8,8]{0,1:T(8,128)S(1)} all-reduce(f32[8,8]{0,1:T(8,128)S(1)} %convolution_bitcast_fusion.5), channel_id=1, replica_groups=mesh['grp'=2,'aux'=8,'tr'=2] {'aux','tr'}, use_global_device_ids=true, to_apply=%region_10.11 | all-reduce | flops 64 | bytes 512 | tf_op jit(solution)/shard_map/psum | solution.py:70
  243.5 30.8 %all_gather.7 = bf16[64,8,256]{2,1,0:T(8,128)(2,1)S(1)} all-gather(bf16[8,8,256]{2,1,0:T(8,128)(2,1)S(1)} %get-tuple-element.150), channel_id=1, replica_groups=mesh['grp'=2,'aux'=8,'tr'=2] {'aux'}, dimensions={0}, use_global_device_ids=true | all-gather | bytes 294912 | tf_op jit(solution)/shard_map/all_gather | solution.py:13
  274.3 46.6 %while.21 = (s32[]{:T(128)}, f32[64,8,512]{2,1,0:T(8,128)S(1)}, s32[]{:T(128)}, bf16[64,64,64]{2,1,0:T(8,128)(2,1)}, bf16[64,8,256]{2,1,0:T(8,128)(2,1)S(1)}, /*...) while((s32[]{:T(128)}, f32[64,8,512]{2,1,0:T(8,128)S(1)}, ...), condition=%wide.region_12.13_spmd, body=%wide.region_11.12_spmd.sunk | while | flops 1210318848 | bytes 12976363 | solution.py:40
  276.0 4.2 fusion.84
  281.8 4.2 fusion.84
  293.4 4.2 fusion.84
  305.1 4.2 fusion.84
  316.7 4.2 fusion.84
  322.0 16.4 %reduce-scatter.9.cloned.1.call-done = f32[64,8,256]{2,1,0:T(8,128)} async-done(((f32[64,8,512]{2,1,0:T(8,128)}), f32[64,8,256]{2,1,0:T(8,128)}) %reduce-scatter.9.cloned.1.call-update) | async-done | bytes 524304 | tf_op jit(solution)/shard_map/reduce_scatter | solution.py:41
  338.4 76.0 %psum.38 = bf16[8,512]{1,0:T(8,128)(2,1)S(1)} all-reduce(f32[8,512]{1,0:T(8,128)S(1)} %get-tuple-element.308), channel_id=1, replica_groups=mesh['grp'=2,'aux'=8,'tr'=2] {'aux','tr'}, use_global_device_ids=true, to_apply=%region_17.18 | all-reduce | flops 4096 | bytes 24576 | tf_op jit(solution)/shard_map/psum | solution.py:49
  416.6 13.1 %all-reduce.5.cloned.1.call-done = f32[8,8,256]{2,1,0:T(8,128)} async-done(((f32[8,8,256]{2,1,0:T(8,128)}), f32[8,8,256]{2,1,0:T(8,128)}) %all-reduce.5.cloned.1.call-update) | async-done | bytes 65552 | tf_op jit(solution)/shard_map/psum | solution.py:58
  (80 shorter events, 48.9 us)
Async XLA Ops:
  7.2 100.8 %reduce-scatter.5.cloned.1.call-start = ((), (), s32[]{:S(2)}) async-start(), calls=%async_computation.4 | async-start | bytes 1572864 | tf_op jit(solution)/shard_map/reduce_scatter | solution.py:41
  41.4 66.7 %copy-start = (bf16[8,256,512]{2,1,0:T(8,128)(2,1)S(1)}, bf16[8,256,512]{2,1,0:T(8,128)(2,1)}, u32[]{:S(2)}) copy-start(bf16[8,256,512]{2,1,0:T(8,128)(2,1)} %param.24) | copy-start | bytes 6291460
  88.1 1.0 copy-start.2
  89.1 94.8 %reduce-scatter.7.cloned.1.call-start = ((), (), s32[]{:S(2)}) async-start(), calls=%async_computation.5 | async-start | bytes 589824 | tf_op jit(solution)/shard_map/reduce_scatter | solution.py:42
  108.0 91.2 %all-reduce.3.cloned.1.call-start = ((), (), s32[]{:S(2)}) async-start(), calls=%async_computation.6 | async-start | bytes 131072 | tf_op jit(solution)/shard_map/psum | solution.py:58
  108.1 77.5 %copy-start.4 = (f32[256]{0:T(256)S(1)}, f32[256]{0:T(256)}, u32[]{:S(2)}) copy-start(f32[256]{0:T(256)} %param.21) | copy-start | bytes 3076
  108.1 77.5 %copy-start.5 = (f32[8]{0:T(128)S(1)}, f32[8]{0:T(128)}, u32[]{:S(2)}) copy-start(f32[8]{0:T(128)} %param.20) | copy-start | bytes 100
  108.1 91.1 %copy-start.3 = (f32[8,8,256]{2,1,0:T(8,128)S(1)}, f32[8,8,256]{2,1,0:T(8,128)}, u32[]{:S(2)}) copy-start(f32[8,8,256]{2,1,0:T(8,128)} %param.19) | copy-start | bytes 196612
  185.5 152.9 %reduce-scatter.9.cloned.1.call-start = ((), (), s32[]{:S(2)}) async-start(), calls=%async_computation.7 | async-start | bytes 1572864 | tf_op jit(solution)/shard_map/reduce_scatter | solution.py:41
  320.9 1.0 copy-start.1
  321.9 92.5 %reduce-scatter.11.cloned.1.call-start = ((), (), s32[]{:S(2)}) async-start(), calls=%async_computation.8 | async-start | bytes 589824 | tf_op jit(solution)/shard_map/reduce_scatter | solution.py:42
  338.4 91.3 %all-reduce.5.cloned.1.call-start = ((), (), s32[]{:S(2)}) async-start(), calls=%async_computation.9 | async-start | bytes 131072 | tf_op jit(solution)/shard_map/psum | solution.py:58
Sparse Core Ops, SparseCore 0:
  89.3 18.6 reduce-scatter.4
  111.3 62.6 reduce-scatter.6
  185.6 13.5 all-reduce.2
  322.0 16.2 reduce-scatter.8
  341.5 62.6 reduce-scatter.10
  416.0 13.5 all-reduce.4
where the time goes:
time: 439 us; the launch traced here: 438 us
  blocking collectives  257 us (59%)
  matrix products  94.6 us (22%)
  waiting for transfers between devices  61.9 us (14%)
  between operations  14.9 us (3%)
  other arithmetic  5.46 us (1%)
    psum x2, blocking collectives, apply_hamiltonian(): projection = lax.psum(projection, ('aux', 'tr'))  152 us
    dot_general x16, matrix products, one_block(): jnp.einsum('pukc,pcd->ukd', blended, piece_virt, preferred_element_type=j...  67 us
    all_gather x2, blocking collectives, apply_hamiltonian(): gathered = lax.all_gather(rounded, 'aux', axis=0, tiled=True)  63.3 us
    psum x1, blocking collectives, body(): intersection = lax.psum(partial_intersection, ('aux', 'tr')) / (V * C)  42.1 us
    reduce_scatter x2, waiting for transfers between devices, apply_hamiltonian(): lax.psum_scatter(direct_term, 'tr', scatter_dimension=2, tiled=True)  35.1 us
    psum x2, waiting for transfers between devices, apply_hamiltonian(): combined = lax.psum(direct_term + exchange_term, 'grp')  26.7 us
    dot_general x16, matrix products, one_block(): jnp.einsum('puv,vkc->pukc', piece_occ, gathered, preferred_element_type=j...  25.6 us
  transfers between devices with their start and end apart: 6, of which 4 were waited for; matrix products, arithmetic and copies ran while one was open for 0% of the time, Pallas kernels for 0%

commit v1 on v0

--- a/solution.py
+++ b/solution.py
@@ -1,3 +1,4 @@
+import functools
 import math
 import jax
 import jax.numpy as jnp
@@ -6,6 +7,14 @@
 
 V = 64
 C = 512
+
+
+def order_map_now(s0, comm_axis):
+    m_next = lax.all_gather(s0, comm_axis)
+    return jnp.sum(m_next, 0)
+
+
+zones_arrange = functools.partial(order_map_now, comm_axis=("aux", "tr"))
 
 
 def apply_hamiltonian(vectors, energy_gap, coef_occ, coef_virt, pair_coef, live_aux):
@@ -67,7 +76,7 @@
     partial_intersection = jnp.einsum(
         "vkc,vjc->kj", trial_vectors, applied_first, precision=lax.Precision.HIGHEST
     )
-    intersection = lax.psum(partial_intersection, ("aux", "tr")) / (V * C)
+    intersection = zones_arrange(partial_intersection) / (V * C)
     residual = applied_first - jnp.einsum(
         "vkc,kj->vjc", trial_vectors, intersection, precision=lax.Precision.HIGHEST
     )

time: 439 us -> 420 us (0.957)
  matrix products: 94.6 us -> 75.8 us
    psum x1 -> x0, blocking collectives: 42.1 us -> none  [body(): intersection = lax.psum(partial_intersection, ('aux', 'tr')) / (V * C)]
    all_gather x0 -> x1, blocking collectives: none -> 41.4 us  [order_map_now(): m_next = lax.all_gather(s0, comm_axis)]
    dot_general x16, matrix products: 67 us -> 48.1 us  [one_block(): jnp.einsum('pukc,pcd->ukd', blended, piece_virt, preferred_element_type=j...]
where the time goes in v1:
time: 420 us; the launch traced here: 419 us
  blocking collectives  256 us (61%)
  matrix products  75.8 us (18%)
  waiting for transfers between devices  61.9 us (15%)
  between operations  15 us (4%)
  other arithmetic  5.47 us (1%)
    psum x2, blocking collectives, apply_hamiltonian(): projection = lax.psum(projection, ('aux', 'tr'))  152 us
    all_gather x2, blocking collectives, apply_hamiltonian(): gathered = lax.all_gather(rounded, 'aux', axis=0, tiled=True)  63.3 us
    dot_general x16, matrix products, one_block(): jnp.einsum('pukc,pcd->ukd', blended, piece_virt, preferred_element_type=j...  48.1 us
    all_gather x1, blocking collectives, order_map_now(): m_next = lax.all_gather(s0, comm_axis)  41.4 us
    reduce_scatter x2, waiting for transfers between devices, apply_hamiltonian(): lax.psum_scatter(direct_term, 'tr', scatter_dimension=2, tiled=True)  35.1 us
    psum x2, waiting for transfers between devices, apply_hamiltonian(): combined = lax.psum(direct_term + exchange_term, 'grp')  26.7 us
    dot_general x16, matrix products, one_block(): jnp.einsum('puv,vkc->pukc', piece_occ, gathered, preferred_element_type=j...  25.6 us
  transfers between devices with their start and end apart: 6, of which 4 were waited for; matrix products, arithmetic and copies ran while one was open for 0% of the time, Pallas kernels for 0%

profile of v1, /device:TPU:0, one launch (start us, length us, event | category | flops | bytes accessed | tf_op | source)
XLA Modules:
  0.0 418.6 jit_solution(15391384696929211790)
XLA Ops:
  8.7 32.5 %all_gather.12 = bf16[64,8,256]{2,1,0:T(8,128)(2,1)S(1)} all-gather(bf16[8,8,256]{2,1,0:T(8,128)(2,1)S(1)} %convert_element_type.40), channel_id=1, replica_groups=mesh['grp'=2,'aux'=8,'tr'=2] {'aux'}, dimensions={0}, use_global_device_ids=true | all-gather | bytes 294912 | tf_op jit(solution)/shard_map/all_gather | solution.py:22
  41.5 37.3 %while.20 = (s32[]{:T(128)}, f32[64,8,512]{2,1,0:T(8,128)S(1)}, s32[]{:T(128)}, bf16[64,64,64]{2,1,0:T(8,128)(2,1)}, bf16[64,8,256]{2,0,1:T(8,128)(2,1)S(1)}, /*...) while((s32[]{:T(128)}, f32[64,8,512]{2,1,0:T(8,128)S(1)}, ...), condition=%wide.region_1.2_spmd, body=%wide.region_0.1_spmd.sunk | while | flops 1210318848 | bytes 8782059 | solution.py:49
  43.2 3.0 fusion.69
  47.9 3.0 fusion.69
  57.2 3.0 fusion.69
  61.8 3.0 fusion.69
  71.1 3.0 fusion.69
  75.8 3.0 fusion.69
  79.8 18.8 %reduce-scatter.5.cloned.1.call-done = f32[64,8,256]{2,1,0:T(8,128)} async-done(((f32[64,8,512]{2,1,0:T(8,128)}), f32[64,8,256]{2,1,0:T(8,128)}) %reduce-scatter.5.cloned.1.call-update) | async-done | bytes 524304 | tf_op jit(solution)/shard_map/reduce_scatter | solution.py:50
  98.7 75.8 %psum.28 = bf16[8,512]{1,0:T(8,128)(2,1)S(1)} all-reduce(f32[8,512]{1,0:T(8,128)S(1)} %get-tuple-element.318), channel_id=1, replica_groups=mesh['grp'=2,'aux'=8,'tr'=2] {'aux','tr'}, use_global_device_ids=true, to_apply=%region_6.7 | all-reduce | flops 4096 | bytes 24576 | tf_op jit(solution)/shard_map/psum | solution.py:58
  176.2 13.6 %all-reduce.3.cloned.1.call-done = f32[8,8,256]{2,1,0:T(8,128)} async-done(((f32[8,8,256]{2,1,0:T(8,128)}), f32[8,8,256]{2,1,0:T(8,128)}) %all-reduce.3.cloned.1.call-update) | async-done | bytes 65552 | tf_op jit(solution)/shard_map/psum | solution.py:67
  190.9 41.4 %all-gather = f32[128,8]{1,0:T(8,128)S(1)} all-gather(f32[8,8]{1,0:T(8,128)S(1)} %copy.14), channel_id=2, replica_groups=mesh['grp'=2,'aux'=8,'tr'=2] {'aux','tr'}, dimensions={0}, use_global_device_ids=true | all-gather | bytes 4352 | tf_op jit(solution)/shard_map/all_gather | solution.py:13
  233.4 30.8 %all_gather.15 = bf16[64,8,256]{2,1,0:T(8,128)(2,1)S(1)} all-gather(bf16[8,8,256]{2,1,0:T(8,128)(2,1)S(1)} %get-tuple-element.162), channel_id=1, replica_groups=mesh['grp'=2,'aux'=8,'tr'=2] {'aux'}, dimensions={0}, use_global_device_ids=true | all-gather | bytes 294912 | tf_op jit(solution)/shard_map/all_gather | solution.py:22
  264.4 37.2 %while.21 = (s32[]{:T(128)}, f32[64,8,512]{2,1,0:T(8,128)S(1)}, s32[]{:T(128)}, bf16[64,64,64]{2,1,0:T(8,128)(2,1)}, bf16[64,8,256]{2,0,1:T(8,128)(2,1)S(1)}, /*...) while((s32[]{:T(128)}, f32[64,8,512]{2,1,0:T(8,128)S(1)}, ...), condition=%wide.region_12.13_spmd, body=%wide.region_11.12_spmd.sunk | while | flops 1210318848 | bytes 8782059 | solution.py:49
  266.0 3.0 fusion.74
  275.3 3.0 fusion.74
  279.9 3.0 fusion.74
  284.6 3.0 fusion.74
  289.2 3.0 fusion.74
  293.9 3.0 fusion.74
  298.5 3.0 fusion.74
  302.6 16.4 %reduce-scatter.9.cloned.1.call-done = f32[64,8,256]{2,1,0:T(8,128)} async-done(((f32[64,8,512]{2,1,0:T(8,128)}), f32[64,8,256]{2,1,0:T(8,128)}) %reduce-scatter.9.cloned.1.call-update) | async-done | bytes 524304 | tf_op jit(solution)/shard_map/reduce_scatter | solution.py:50
  319.0 76.0 %psum.30 = bf16[8,512]{1,0:T(8,128)(2,1)S(1)} all-reduce(f32[8,512]{1,0:T(8,128)S(1)} %get-tuple-element.320), channel_id=1, replica_groups=mesh['grp'=2,'aux'=8,'tr'=2] {'aux','tr'}, use_global_device_ids=true, to_apply=%region_17.18 | all-reduce | flops 4096 | bytes 24576 | tf_op jit(solution)/shard_map/psum | solution.py:58
  397.2 13.1 %all-reduce.5.cloned.1.call-done = f32[8,8,256]{2,1,0:T(8,128)} async-done(((f32[8,8,256]{2,1,0:T(8,128)}), f32[8,8,256]{2,1,0:T(8,128)}) %all-reduce.5.cloned.1.call-update) | async-done | bytes 65552 | tf_op jit(solution)/shard_map/psum | solution.py:67
  (85 shorter events, 45.7 us)
Async XLA Ops:
  7.2 91.4 %reduce-scatter.5.cloned.1.call-start = ((), (), s32[]{:S(2)}) async-start(), calls=%async_computation.4 | async-start | bytes 1572864 | tf_op jit(solution)/shard_map/reduce_scatter | solution.py:50
  41.5 57.2 %copy-start = (bf16[8,256,512]{2,1,0:T(8,128)(2,1)S(1)}, bf16[8,256,512]{2,1,0:T(8,128)(2,1)}, u32[]{:S(2)}) copy-start(bf16[8,256,512]{2,1,0:T(8,128)(2,1)} %param.24) | copy-start | bytes 6291460
  78.8 1.0 copy-start.2
  79.8 94.8 %reduce-scatter.7.cloned.1.call-start = ((), (), s32[]{:S(2)}) async-start(), calls=%async_computation.5 | async-start | bytes 589824 | tf_op jit(solution)/shard_map/reduce_scatter | solution.py:51
  98.6 91.2 %all-reduce.3.cloned.1.call-start = ((), (), s32[]{:S(2)}) async-start(), calls=%async_computation.6 | async-start | bytes 131072 | tf_op jit(solution)/shard_map/psum | solution.py:67
  98.7 77.5 %copy-start.4 = (f32[256]{0:T(256)S(1)}, f32[256]{0:T(256)}, u32[]{:S(2)}) copy-start(f32[256]{0:T(256)} %param.21) | copy-start | bytes 3076
  98.7 77.5 %copy-start.5 = (f32[8]{0:T(128)S(1)}, f32[8]{0:T(128)}, u32[]{:S(2)}) copy-start(f32[8]{0:T(128)} %param.20) | copy-start | bytes 100
  98.7 91.1 %copy-start.3 = (f32[8,8,256]{2,1,0:T(8,128)S(1)}, f32[8,8,256]{2,1,0:T(8,128)}, u32[]{:S(2)}) copy-start(f32[8,8,256]{2,1,0:T(8,128)} %param.19) | copy-start | bytes 196612
  176.1 142.9 %reduce-scatter.9.cloned.1.call-start = ((), (), s32[]{:S(2)}) async-start(), calls=%async_computation.7 | async-start | bytes 1572864 | tf_op jit(solution)/shard_map/reduce_scatter | solution.py:50
  301.5 1.0 copy-start.1
  302.5 92.5 %reduce-scatter.11.cloned.1.call-start = ((), (), s32[]{:S(2)}) async-start(), calls=%async_computation.8 | async-start | bytes 589824 | tf_op jit(solution)/shard_map/reduce_scatter | solution.py:51
  319.0 91.3 %all-reduce.5.cloned.1.call-start = ((), (), s32[]{:S(2)}) async-start(), calls=%async_computation.9 | async-start | bytes 131072 | tf_op jit(solution)/shard_map/psum | solution.py:67
Sparse Core Ops, SparseCore 0:
  79.9 18.6 reduce-scatter.4
  101.9 62.7 reduce-scatter.6
  176.2 13.5 all-reduce.2
  302.6 16.2 reduce-scatter.8
  322.1 62.6 reduce-scatter.10
  396.6 13.5 all-reduce.4
